TPU v7x, 512 devices: a whole 4x8x8 slice. The times are simulated.
512 devices in a mesh: section: 16 (over x, y_lo, core), tensor: 32 (over y_hi, z).
Axes of the slice: x: 4, y: 8 (y_hi: 4, y_lo: 2; y = y_hi * 2 + y_lo), z: 8, core: 2. Of those that a mesh axis runs over, the one named last changes fastest.
Arguments:
- hidden: bfloat16 [16, 256, 8192], P('section', 'tensor'), may hold values from -60 to 60
- norm_gain: float32 [8192], replicated, may hold values from 0.1 to 1.9
- lengths: int32 [16], P('section'), may hold values from 64 to 256
- query_param: float32 [8192, 4096], P(('section', 'tensor')), may hold values from -1.3258252 to 1.3258252
- query_grad: float32 [8192, 4096], P(('section', 'tensor')), may hold values from -0.006 to 0.006
- query_moment: float32 [8192, 4096], P(('section', 'tensor')), may hold values from -0.006 to 0.006
- query_second: float32 [8192, 4096], P(('section', 'tensor')), may hold values from 1e-07 to 1e-05
- keyval_param: float32 [8192, 1024], P(('section', 'tensor')), may hold values from -0.06629126 to 0.06629126
- keyval_gradient: float32 [8192, 1024], P(('section', 'tensor')), may hold values from -0.006 to 0.006
- keyval_first_moment: float32 [8192, 1024], P(('section', 'tensor')), may hold values from -0.006 to 0.006
- keyval_second_moment: float32 [8192, 1024], P(('section', 'tensor')), may hold values from 1e-07 to 1e-05
- output_param: float32 [8192, 4096], P(('section', 'tensor')), may hold values from -0.25 to 0.25
- output_grad: float32 [8192, 4096], P(('section', 'tensor')), may hold values from -0.006 to 0.006
- output_moment: float32 [8192, 4096], P(('section', 'tensor')), may hold values from -0.006 to 0.006
- output_second: float32 [8192, 4096], P(('section', 'tensor')), may hold values from 1e-07 to 1e-05
Outputs:
- mixed: bfloat16 [16, 256, 8192], P('section', 'tensor')
All inputs are finite; a program needn't handle non-finite values.
Results may differ from a plain program's by a relative error of at most 0.017.
Values may be sent and summed in bfloat16 or wider, within the bound.
No kernel may reach another device: no remote copies, remote signals or barrier semaphores. Data moves between devices by JAX's collectives and lax.ppermute only.
A program may use at most 64 MiB of HBM per device.

v0:
```python
import math
import jax
import jax.numpy as jnp
from jax import lax
from jax.sharding import PartitionSpec as P

QUERY_HEADS_LOCAL = 32
KEYVAL_HEADS = 4
HEAD_DIMENSION = 128
learn_rate = 0.015
beta_one = 0.5
beta_two = 0.9
adam_step = 1000.0
adam_eps = 1e-08
decay_rate = 0.1
norm_eps = 1e-06
rope_base = 1000000.0
masked_score = -1e30


def adam_update(current, gradient, moment, second):
    moment_new = beta_one * moment + (1.0 - beta_one) * gradient
    second_new = beta_two * second + (1.0 - beta_two) * gradient * gradient
    corrected = moment_new / (1.0 - beta_one**adam_step)
    denominator = jnp.sqrt(second_new / (1.0 - beta_two**adam_step)) + adam_eps
    return (current - learn_rate * (corrected / denominator + decay_rate * current)).astype(
        jnp.bfloat16
    )


def normalize(hidden, norm_gain):
    values = hidden.astype(jnp.float32)
    factor = lax.rsqrt(jnp.mean(values * values, axis=-1, keepdims=True) + norm_eps)
    return (values * factor * norm_gain).astype(jnp.bfloat16)


def rotary_embed(values, token_positions):
    half_width = values.shape[-1] // 2
    frequency = rope_base ** (-jnp.arange(half_width, dtype=jnp.float32) * 2.0 / values.shape[-1])
    angles = token_positions.astype(jnp.float32)[:, None] * frequency[None, :]
    cosine_table = jnp.concatenate([jnp.cos(angles), jnp.cos(angles)], axis=-1)
    sine_table = jnp.concatenate([jnp.sin(angles), jnp.sin(angles)], axis=-1)
    first_half = values[..., :half_width]
    second_half = values[..., half_width:]
    rotated = jnp.concatenate([-second_half, first_half], axis=-1)
    return values * cosine_table + rotated * sine_table


def on_device(
    hidden,
    norm_gain,
    lengths,
    query_param,
    query_grad,
    query_moment,
    query_second,
    keyval_param,
    keyval_gradient,
    keyval_first_moment,
    keyval_second_moment,
    output_param,
    output_grad,
    output_moment,
    output_second,
):
    tensor_count = lax.axis_size("tensor")
    query_weight = adam_update(query_param, query_grad, query_moment, query_second)
    keyval_matrix = adam_update(
        keyval_param, keyval_gradient, keyval_first_moment, keyval_second_moment
    )
    output_weight = adam_update(output_param, output_grad, output_moment, output_second)
    local_rows = normalize(hidden[0], norm_gain)
    normed = lax.all_gather(local_rows, "tensor", axis=0, tiled=True)
    sequence = normed.shape[0]
    model_width = normed.shape[1]
    weight_row_block = query_weight.shape[0]
    heads_here = QUERY_HEADS_LOCAL // tensor_count
    head_columns = heads_here * HEAD_DIMENSION
    head_copies = tensor_count // KEYVAL_HEADS
    spread_heads = keyval_matrix.reshape(weight_row_block, 2, KEYVAL_HEADS, HEAD_DIMENSION)
    spread_heads = (
        jnp.repeat(spread_heads, head_copies, axis=2)
        .transpose(0, 2, 1, 3)
        .reshape(weight_row_block, tensor_count * 2 * HEAD_DIMENSION)
    )
    keyval_columns = spread_heads.shape[1] // tensor_count
    query_start = jnp.zeros((sequence, head_columns), jnp.float32)
    keyval_start = jnp.zeros((sequence, keyval_columns), jnp.float32)
    query_slice, keyval_slice, output_slice = (
        lax.all_to_all(query_weight, "tensor", split_axis=1, concat_axis=0, tiled=True),
        lax.all_to_all(spread_heads, "tensor", split_axis=1, concat_axis=0, tiled=True),
        lax.all_to_all(output_weight, "tensor", split_axis=1, concat_axis=0, tiled=True),
    )
    initial = (query_start, keyval_start, jnp.zeros((model_width, head_columns), jnp.bfloat16))
    offset = jnp.int32(0)
    query_total = initial[0]
    query_rows = lax.all_gather(query_slice, "section", axis=0, tiled=True)
    keyval_rows = lax.all_gather(keyval_slice, "section", axis=0, tiled=True)
    columns = lax.dynamic_slice_in_dim(normed, offset, query_rows.shape[0], 1)
    query_total = query_total + jnp.dot(columns, query_rows, preferred_element_type=jnp.float32)
    keyval_total = jnp.dot(columns, keyval_rows, preferred_element_type=jnp.float32)
    query_total, keyval_total = (query_total, keyval_total)
    out_buffer = lax.dynamic_update_slice_in_dim(
        initial[2], lax.all_gather(output_slice, "section", axis=0, tiled=True), offset, 0
    )
    key_block = keyval_total[:, :HEAD_DIMENSION]
    value_block = keyval_total[:, HEAD_DIMENSION:]
    token_positions = jnp.arange(sequence)
    query_heads = rotary_embed(
        query_total.reshape(sequence, heads_here, HEAD_DIMENSION).transpose(1, 0, 2),
        token_positions,
    ).astype(jnp.bfloat16)
    key_head_rows = rotary_embed(key_block, token_positions).astype(jnp.bfloat16)
    value_head_rows = value_block.astype(jnp.bfloat16)
    scores = jnp.einsum(
        "hqd,kd->hqk", query_heads, key_head_rows, preferred_element_type=jnp.float32
    ) / math.sqrt(HEAD_DIMENSION)
    allowed = (token_positions[None, :] <= token_positions[:, None]) & (
        token_positions[None, :] < lengths[0]
    )
    scores = jnp.where(allowed[None], scores, masked_score)
    row_max = jnp.max(scores, axis=-1, keepdims=True)
    exponent = jnp.exp(scores - row_max)
    attention = (exponent / jnp.sum(exponent, axis=-1, keepdims=True)).astype(jnp.bfloat16)
    head_out = jnp.einsum(
        "hqk,kd->hqd", attention, value_head_rows, preferred_element_type=jnp.float32
    ).astype(jnp.bfloat16)
    head_out = head_out.transpose(1, 0, 2).reshape(sequence, head_columns)
    mixed = lax.psum_scatter(
        lax.dot_general(
            head_out, out_buffer, (((1,), (1,)), ((), ())), preferred_element_type=jnp.float32
        ).astype(jnp.bfloat16),
        "tensor",
        scatter_dimension=0,
        tiled=True,
    )
    return mixed[None]


def solution(mesh):
    return jax.shard_map(
        on_device,
        mesh=mesh,
        in_specs=(
            P("section", "tensor", None),
            P(),
            P("section"),
            P(("section", "tensor"), None),
            P(("section", "tensor"), None),
            P(("section", "tensor"), None),
            P(("section", "tensor"), None),
            P(("section", "tensor"), None),
            P(("section", "tensor"), None),
            P(("section", "tensor"), None),
            P(("section", "tensor"), None),
            P(("section", "tensor"), None),
            P(("section", "tensor"), None),
            P(("section", "tensor"), None),
            P(("section", "tensor"), None),
        ),
        out_specs=P("section", "tensor", None),
        check_vma=False,
    )
```

profile of v0, /device:TPU:2, one launch (start us, length us, event | category | flops | bytes accessed | tf_op | source)
XLA Modules:
  0.0 503.8 jit_solution(8124403716524646474)
XLA Ops:
  6.5 0.0 all-gather.7.cloned.1.call-start
  6.6 1.5 copy_bitcast_fusion.1
  8.0 28.5 %all_to_all.57 = bf16[16,32,128]{2,0,1:T(8,128)(2,1)} all-to-all(bf16[16,32,128]{2,0,1:T(8,128)(2,1)S(1)} %copy_bitcast_fusion.1), channel_id=1, replica_groups=mesh['section'=16,'tensor'=32] {'tensor'}, dimensions={1} | all-to-all | bytes 262144 | tf_op jit(solution)/shard_map/all_to_all | solution.py:90
  36.5 0.0 all-gather.7.cloned.1.call-update
  36.5 0.0 all-gather.5.cloned.1.call-start
  36.6 1.1 fusion.1
  37.7 1.7 fusion.3
  39.3 0.0 all-gather.5.cloned.1.call-update
  39.4 0.0 all-gather.9.cloned.1.call-start
  39.4 1.0 fusion.44
  40.5 0.1 broadcast_in_dim.7
  40.6 0.2 all_to_all.46
  40.8 0.2 copy.24
  41.0 17.3 %all_to_all.58 = bf16[16,32,256]{2,0,1:T(8,128)(2,1)} all-to-all(bf16[16,32,256]{2,0,1:T(8,128)(2,1)S(1)} %copy.24), channel_id=1, replica_groups=mesh['section'=16,'tensor'=32] {'tensor'}, dimensions={1} | all-to-all | bytes 524288 | tf_op jit(solution)/shard_map/all_to_all | solution.py:91
  58.2 0.0 all-gather.9.cloned.1.call-update
  58.3 0.0 all-gather.11.cloned.1.call-start
  58.4 0.2 copy_bitcast_fusion
  58.6 16.7 %all_to_all.59 = bf16[16,32,128]{2,0,1:T(8,128)(2,1)} all-to-all(bf16[16,32,128]{2,0,1:T(8,128)(2,1)S(1)} %copy_bitcast_fusion), channel_id=1, replica_groups=mesh['section'=16,'tensor'=32] {'tensor'}, dimensions={1} | all-to-all | bytes 262144 | tf_op jit(solution)/shard_map/all_to_all | solution.py:92
  75.3 0.0 all-gather.11.cloned.1.call-update
  75.3 0.0 reduce-scatter.2.cloned.1.call-start
  76.0 0.3 multiply_sine_fusion
  76.3 0.0 all-gather.7.cloned.1.call-done
  76.4 100.0 %all-gather.5.cloned.1.call-done = bf16[256,8192]{1,0:T(8,128)(2,1)} async-done(((bf16[8,8192]{1,0:T(8,128)(2,1)}), bf16[256,8192]{1,0:T(8,128)(2,1)}) %all-gather.5.cloned.1.call-update) | async-done | bytes 4194320 | tf_op jit(solution)/shard_map/all_gather | solution.py:73
  176.4 4.4 fusion.47
  180.7 35.5 %all-gather.9.cloned.1.call-done = bf16[8192,256]{1,0:T(8,128)(2,1)} async-done(((bf16[512,256]{1,0:T(8,128)(2,1)}), bf16[8192,256]{1,0:T(8,128)(2,1)}) %all-gather.9.cloned.1.call-update) | async-done | bytes 4194320 | tf_op jit(solution)/shard_map/all_gather | solution.py:98
  216.2 5.2 %fusion.48 = f32[256,256]{0,1:T(8,128)S(1)} fusion(bf16[256,8192]{1,0:T(8,128)(2,1)} %all-gather.5.cloned.1.call-done, bf16[8192,256]{1,0:T(8,128)(2,1)} %all-gather.9.cloned.1.call-done), kind=kOutput, calls=%fused_computation.71 | convolution fusion | flops 1073741824 | bytes 8650752 | tf_op jit(solution)/shard_map/dot_general | solution.py:101
  221.4 0.3 fusion.46
  221.7 0.1 fusion.21
  221.8 35.8 %all-gather.11.cloned.1.call-done = bf16[8192,128]{1,0:T(8,128)(2,1)} async-done(((bf16[512,128]{1,0:T(8,128)(2,1)}), bf16[8192,128]{1,0:T(8,128)(2,1)}) %all-gather.11.cloned.1.call-update) | async-done | bytes 2097168 | tf_op jit(solution)/shard_map/all_gather | solution.py:104
  257.5 5.0 convolution_convert_fusion
  262.5 0.0 reduce-scatter.2.cloned.1.call-update
  262.5 234.8 %reduce-scatter.2.cloned.1.call-done = bf16[8,8192]{1,0:T(8,128)(2,1)} async-done(((bf16[256,8192]{1,0:T(8,128)(2,1)}), bf16[8,8192]{1,0:T(8,128)(2,1)}) %reduce-scatter.2.cloned.1.call-update) | async-done | bytes 131088 | tf_op jit(solution)/shard_map/reduce_scatter | solution.py:129
  (16 shorter events, 0.1 us)
Async XLA Ops:
  6.5 51.8 %copy-start = (f32[16,4096]{1,0:T(8,128)S(1)}, f32[16,4096]{1,0:T(8,128)}, u32[]{:S(2)}) copy-start(f32[16,4096]{1,0:T(8,128)} %param.26) | copy-start | bytes 786436
  6.5 51.8 %copy-start.1 = (f32[16,4096]{1,0:T(8,128)S(1)}, f32[16,4096]{1,0:T(8,128)}, u32[]{:S(2)}) copy-start(f32[16,4096]{1,0:T(8,128)} %param.27) | copy-start | bytes 786436
  6.5 51.8 %copy-start.3 = (f32[16,4096]{1,0:T(8,128)S(1)}, f32[16,4096]{1,0:T(8,128)}, u32[]{:S(2)}) copy-start(f32[16,4096]{1,0:T(8,128)} %param.28) | copy-start | bytes 786436
  6.5 51.8 %copy-start.2 = (f32[16,4096]{1,0:T(8,128)S(1)}, f32[16,4096]{1,0:T(8,128)}, u32[]{:S(2)}) copy-start(f32[16,4096]{1,0:T(8,128)} %param.29) | copy-start | bytes 786436
  6.5 69.8 %all-gather.7.cloned.1.call-start = ((), (), s32[]{:S(2)}) async-start(), calls=%async_computation.5 | async-start | bytes 2228224 | tf_op jit(solution)/shard_map/all_gather | solution.py:97
  36.5 139.8 %all-gather.5.cloned.1.call-start = ((), (), s32[]{:S(2)}) async-start(), calls=%async_computation.4 | async-start | bytes 4325376 | tf_op jit(solution)/shard_map/all_gather | solution.py:73
  39.4 176.8 %all-gather.9.cloned.1.call-start = ((), (), s32[]{:S(2)}) async-start(), calls=%async_computation.6 | async-start | bytes 4456448 | tf_op jit(solution)/shard_map/all_gather | solution.py:98
  58.3 199.3 %all-gather.11.cloned.1.call-start = ((), (), s32[]{:S(2)}) async-start(), calls=%async_computation.7 | async-start | bytes 2228224 | tf_op jit(solution)/shard_map/all_gather | solution.py:104
  75.3 422.0 %reduce-scatter.2.cloned.1.call-start = ((), (), s32[]{:S(2)}) async-start(), calls=%async_computation.8 | async-start | bytes 4325376 | tf_op jit(solution)/shard_map/reduce_scatter | solution.py:129
Sparse Core Ops, SparseCore 0:
  36.7 33.0 all-gather.6
  72.9 103.3 all-gather.4
  178.5 37.6 all-gather.8
  218.2 39.2 all-gather.10
  262.6 234.6 reduce-scatter.1
where the time goes:
time: 504 us
  waiting for transfers between devices  406 us (81%)
  blocking collectives  62.4 us (12%)
  matrix products  14.8 us (3%)
  between operations  13.9 us (3%)
  other arithmetic  5.83 us (1%)
    reduce_scatter x1, waiting for transfers between devices, on_device(): lax.psum_scatter(lax.dot_general(head_out, out_buffer, (((1,), (1,)), (()...  235 us
    all_gather x1, waiting for transfers between devices, on_device(): normed = lax.all_gather(local_rows, 'tensor', axis=0, tiled=True)  100 us
    all_gather x1, waiting for transfers between devices, on_device(): lax.all_gather(output_slice, 'section', axis=0, tiled=True)  35.8 us
    all_gather x1, waiting for transfers between devices, on_device(): keyval_rows = lax.all_gather(keyval_slice, 'section', axis=0, tiled=True)  35.5 us
    all_to_all x1, blocking collectives, on_device(): lax.all_to_all(query_weight, 'tensor', split_axis=1, concat_axis=0, tiled...  28.5 us
    all_to_all x1, blocking collectives, on_device(): lax.all_to_all(spread_heads, 'tensor', split_axis=1, concat_axis=0, tiled...  17.3 us
    all_to_all x1, blocking collectives, on_device(): lax.all_to_all(output_weight, 'tensor', split_axis=1, concat_axis=0, tile...  16.7 us
  transfers between devices with their start and end apart: 5, of which 4 were waited for; matrix products, arithmetic and copies ran while one was open for 3% of the time, Pallas kernels for 0%

commit v1 on v0

--- a/solution.py
+++ b/solution.py
@@ -95,7 +95,8 @@
     offset = jnp.int32(0)
     query_total = initial[0]
     query_rows = lax.all_gather(query_slice, "section", axis=0, tiled=True)
-    keyval_rows = lax.all_gather(keyval_slice, "section", axis=0, tiled=True)
+    stack = jnp.stack([keyval_slice] * lax.axis_size("section"))
+    keyval_rows = jnp.concatenate(lax.all_to_all(stack, "section", 0, 0), axis=0)
     columns = lax.dynamic_slice_in_dim(normed, offset, query_rows.shape[0], 1)
     query_total = query_total + jnp.dot(columns, query_rows, preferred_element_type=jnp.float32)
     keyval_total = jnp.dot(columns, keyval_rows, preferred_element_type=jnp.float32)

time: 504 us -> 461 us (0.915)
  waiting for transfers between devices: 406 us -> 365 us
  blocking collectives: 62.4 us -> 44.9 us
  starting transfers between devices: 0.2 us -> 11.7 us
    all_gather x1 -> x0, waiting for transfers between devices: 35.5 us -> none  [on_device(): keyval_rows = lax.all_gather(keyval_slice, 'section', axis=0, tiled=True)]
    all_to_all x1 -> x0, blocking collectives: 16.7 us -> none  [on_device(): lax.all_to_all(output_weight, 'tensor', split_axis=1, concat_axis=0, tile...]
    all_to_all x0 -> x2, starting transfers between devices: none -> 11.6 us  [the longest x1 7.73 us: on_device(): lax.all_to_all(stack, 'section', 0, 0)]
    all_to_all x0 -> x2, waiting for transfers between devices: none -> 11.2 us  [the longest x1 11.1 us: on_device(): lax.all_to_all(output_weight, 'tensor', split_axis=1, concat_axis=0, tile...]
    all_gather x1, waiting for transfers between devices: 35.8 us -> 26.9 us  [on_device(): lax.all_gather(output_slice, 'section', axis=0, tiled=True)]
    all_gather x1, waiting for transfers between devices: 100 us -> 91.6 us  [on_device(): normed = lax.all_gather(local_rows, 'tensor', axis=0, tiled=True)]
  transfers between devices with their start and end apart: 5 -> 6, of which waited for: 4 -> 4; matrix products, arithmetic and copies ran while one was open for 3% -> 4% of each run, Pallas kernels for 0% -> 0%
where the time goes in v1:
time: 461 us
  waiting for transfers between devices  365 us (79%)
  blocking collectives  44.9 us (10%)
  matrix products  14.8 us (3%)
  between operations  13.9 us (3%)
  starting transfers between devices  11.7 us (3%)
  other arithmetic  7.59 us (2%)
    reduce_scatter x1, waiting for transfers between devices, on_device(): lax.psum_scatter(lax.dot_general(head_out, out_buffer, (((1,), (1,)), (()...  235 us
    all_gather x1, waiting for transfers between devices, on_device(): normed = lax.all_gather(local_rows, 'tensor', axis=0, tiled=True)  91.6 us
    all_to_all x1, blocking collectives, on_device(): lax.all_to_all(query_weight, 'tensor', split_axis=1, concat_axis=0, tiled...  28.5 us
    all_gather x1, waiting for transfers between devices, on_device(): lax.all_gather(output_slice, 'section', axis=0, tiled=True)  26.9 us
    all_to_all x1, blocking collectives, on_device(): lax.all_to_all(spread_heads, 'tensor', split_axis=1, concat_axis=0, tiled...  16.4 us
    all_to_all x1, waiting for transfers between devices, on_device(): lax.all_to_all(output_weight, 'tensor', split_axis=1, concat_axis=0, tile...  11.1 us
  transfers between devices with their start and end apart: 6, of which 4 were waited for; matrix products, arithmetic and copies ran while one was open for 4% of the time, Pallas kernels for 0%

profile of v1, /device:TPU:2, one launch (start us, length us, event | category | flops | bytes accessed | tf_op | source)
XLA Modules:
  0.0 460.8 jit_solution(16768873458172769386)
XLA Ops:
  6.5 1.4 copy_bitcast_fusion.1
  7.9 28.5 %all_to_all.59 = bf16[16,32,128]{2,0,1:T(8,128)(2,1)} all-to-all(bf16[16,32,128]{2,0,1:T(8,128)(2,1)S(1)} %copy_bitcast_fusion.1), channel_id=1, replica_groups=mesh['section'=16,'tensor'=32] {'tensor'}, dimensions={1} | all-to-all | bytes 262144 | tf_op jit(solution)/shard_map/all_to_all | solution.py:90
  36.4 0.0 all-gather.6.cloned.1.call-update
  36.4 0.0 all-gather.4.cloned.1.call-start
  36.5 1.1 fusion.1
  37.6 1.7 fusion.3
  39.2 0.0 all-gather.4.cloned.1.call-update
  39.2 2.0 copy_bitcast_fusion
  41.3 3.9 all-to-all-start.3
  45.1 1.0 fusion.44
  46.2 0.1 broadcast_in_dim.7
  46.4 0.2 all_to_all.47
  46.5 0.2 copy.24
  46.7 11.1 %all-to-all-done.3 = bf16[16,32,128]{2,0,1:T(8,128)(2,1)S(1)} async-done(((bf16[16,32,128]{2,0,1:T(8,128)(2,1)}), bf16[16,32,128]{2,0,1:T(8,128)(2,1)S(1)}, u32[]{:S(2)}, u32[]{:S(2)}) %all-to-all-start.3) | async-done | bytes 131104 | tf_op jit(solution)/shard_map/all_to_all | solution.py:92
  57.8 16.4 %all_to_all.60 = bf16[16,32,256]{2,0,1:T(8,128)(2,1)S(1)} all-to-all(bf16[16,32,256]{2,0,1:T(8,128)(2,1)S(1)} %copy.24), channel_id=1, replica_groups=mesh['section'=16,'tensor'=32] {'tensor'}, dimensions={1} | all-to-all | bytes 524288 | tf_op jit(solution)/shard_map/all_to_all | solution.py:91
  74.3 2.4 stack.5
  76.6 7.7 %all-to-all-start.2 = ((bf16[16,512,256]{2,1,0:T(8,128)(2,1)}), bf16[16,512,256]{2,1,0:T(8,128)(2,1)}, u32[]{:S(2)}, u32[]{:S(2)}) async-start(bf16[16,512,256]{2,1,0:T(8,128)(2,1)} %stack.5), calls=%async_computation.2 | async-start | bytes 8388608 | tf_op jit(solution)/shard_map/all_to_all | solution.py:99
  84.4 0.0 all-gather.8.cloned.1.call-start
  84.4 0.7 all-gather.8.cloned.1.call-update
  85.1 0.0 reduce-scatter.2.cloned.1.call-start
  85.8 0.3 multiply_sine_fusion
  86.1 0.0 all-gather.6.cloned.1.call-done
  86.2 91.6 %all-gather.4.cloned.1.call-done = bf16[256,8192]{1,0:T(8,128)(2,1)} async-done(((bf16[8,8192]{1,0:T(8,128)(2,1)}), bf16[256,8192]{1,0:T(8,128)(2,1)}) %all-gather.4.cloned.1.call-update) | async-done | bytes 4194320 | tf_op jit(solution)/shard_map/all_gather | solution.py:73
  177.8 4.4 fusion.47
  182.2 0.0 all-to-all-done.2
  182.2 5.2 %fusion.48 = f32[256,256]{0,1:T(8,128)S(1)} fusion(bf16[256,8192]{1,0:T(8,128)(2,1)} %all-gather.4.cloned.1.call-done, bf16[8192,256]{1,0:T(8,128)(2,1)} %bitcast.12), kind=kOutput, calls=%fused_computation.71 | convolution fusion | flops 1073741824 | bytes 8650752 | tf_op jit(solution)/shard_map/dot_general | solution.py:102
  187.4 0.3 fusion.46
  187.7 0.1 fusion.21
  187.8 26.9 %all-gather.8.cloned.1.call-done = bf16[8192,128]{1,0:T(8,128)(2,1)} async-done(((bf16[512,128]{1,0:T(8,128)(2,1)}), bf16[8192,128]{1,0:T(8,128)(2,1)}) %all-gather.8.cloned.1.call-update) | async-done | bytes 2097168 | tf_op jit(solution)/shard_map/all_gather | solution.py:105
  214.6 4.9 %convolution_convert_fusion = bf16[256,8192]{1,0:T(8,128)(2,1)} fusion(bf16[8192,128]{1,0:T(8,128)(2,1)} %all-gather.8.cloned.1.call-done, f32[256,256]{0,1:T(8,128)S(1)} %get-tuple-element.12, f32[256]{0:T(256)S(1)} %fusion.21, f32[256]{0:T(256)S(1)} %get-tuple-element.11, f32[256,256]{0,1:T(8,128)S(1)} %fusion.48), kind=kOutput, calls=%fused_computation | convolution fusion | flops 555974656 | bytes 6621184 | tf_op jit(solution)/shard_map/dot_general | solution.py:131
  219.6 0.0 reduce-scatter.2.cloned.1.call-update
  219.6 234.7 %reduce-scatter.2.cloned.1.call-done = bf16[8,8192]{1,0:T(8,128)(2,1)} async-done(((bf16[256,8192]{1,0:T(8,128)(2,1)}), bf16[8,8192]{1,0:T(8,128)(2,1)}) %reduce-scatter.2.cloned.1.call-update) | async-done | bytes 131088 | tf_op jit(solution)/shard_map/reduce_scatter | solution.py:130
  (11 shorter events, 0.1 us)
Async XLA Ops:
  6.5 79.6 %all-gather.6.cloned.1.call-start = ((), (), s32[]{:S(2)}) async-start(), calls=%async_computation.6 | async-start | bytes 2228224 | tf_op jit(solution)/shard_map/all_gather | solution.py:97
  36.4 141.4 %all-gather.4.cloned.1.call-start = ((), (), s32[]{:S(2)}) async-start(), calls=%async_computation.5 | async-start | bytes 4325376 | tf_op jit(solution)/shard_map/all_gather | solution.py:73
  41.3 16.6 %all-to-all-start.3 = ((bf16[16,32,128]{2,0,1:T(8,128)(2,1)}), bf16[16,32,128]{2,0,1:T(8,128)(2,1)S(1)}, u32[]{:S(2)}, u32[]{:S(2)}) async-start(bf16[16,32,128]{2,0,1:T(8,128)(2,1)} %copy_bitcast_fusion), calls=%async_computation.3 | async-start | bytes 262144 | tf_op jit(solution)/shard_map/all_to_all | solution.py:92
  57.8 18.8 %copy-start = (bf16[16,32,128]{2,0,1:T(8,128)(2,1)}, bf16[16,32,128]{2,0,1:T(8,128)(2,1)S(1)}, u32[]{:S(2)}) copy-start(bf16[16,32,128]{2,0,1:T(8,128)(2,1)S(1)} %all-to-all-done.3) | copy-start | bytes 393220
  76.6 105.6 %all-to-all-start.2 = ((bf16[16,512,256]{2,1,0:T(8,128)(2,1)}), bf16[16,512,256]{2,1,0:T(8,128)(2,1)}, u32[]{:S(2)}, u32[]{:S(2)}) async-start(bf16[16,512,256]{2,1,0:T(8,128)(2,1)} %stack.5), calls=%async_computation.2 | async-start | bytes 8388608 | tf_op jit(solution)/shard_map/all_to_all | solution.py:99
  84.4 130.3 %all-gather.8.cloned.1.call-start = ((), (), s32[]{:S(2)}) async-start(), calls=%async_computation.7 | async-start | bytes 2228224 | tf_op jit(solution)/shard_map/all_gather | solution.py:105
  85.1 369.1 %reduce-scatter.2.cloned.1.call-start = ((), (), s32[]{:S(2)}) async-start(), calls=%async_computation.8 | async-start | bytes 4325376 | tf_op jit(solution)/shard_map/reduce_scatter | solution.py:130
Sparse Core Ops, SparseCore 0:
  36.5 32.4 all-gather.5
  72.2 105.5 all-gather.3
  179.9 34.6 all-gather.7
  219.7 234.4 reduce-scatter.1
